TPU v7x, 32 devices: a whole 2x2x4 slice. The times are simulated.
32 devices in a mesh: gx: 16 (over z, x, core), gy: 2 (over y).
Axes of the slice: x: 2, y: 2, z: 4, core: 2. Of those that a mesh axis runs over, the one named last changes fastest.
Arguments:
- adjoint: bfloat16 [256, 256, 512], P('gx', 'gy'), may hold values from -6 to 6
- conduct_x: float32 [256, 256], P('gx', 'gy'), may hold values from 0.02 to 0.24
- conduct_y: float32 [256, 256], P('gx', 'gy'), may hold values from 0.02 to 0.24
- pick_weights: bfloat16 [64, 256, 256], P(None, 'gx', 'gy'), may hold values from -0.03125 to 0.03125
- owner_order: int32 [64], replicated, may hold values from 0 to 63, each once
Outputs:
- smoothed: bfloat16 [256, 256, 512], P('gx', 'gy')
- representer: float32 [64, 512], P(('gx', 'gy'))
Inputs may be any that keep to these rules, and one draw needn't show every extreme that they name: `owner_order`: each of 0 to 63 appears once.
All inputs are finite; a program needn't handle non-finite values.
Results may differ from a plain program's by a relative error of at most 0.0029.
Values may be sent and summed in bfloat16 or wider, within the bound.
A program may use at most 64 MiB of HBM per device.

v0:
```python
import jax
import jax.numpy as jnp
from jax import lax
from jax.sharding import PartitionSpec as P

PANEL = 256
PANELS = 2
STEPS = 4


def extended(array, sides, width):
    for axis, dim in sides:
        peers, length = (lax.axis_size(axis), array.shape[dim])
        up = [(i, (i + 1) % peers) for i in range(peers - 1)]
        down = [(j, i) for i, j in up]
        last = lax.slice_in_dim(array, length - width, length, axis=dim)
        leading = lax.slice_in_dim(array, 0, width, axis=dim)
        before = lax.ppermute(last, axis, up)
        after = lax.ppermute(leading, axis, down)
        array = jnp.concatenate([before, array, after], axis=dim)
    return array


def diffuse(field, conx, cony):
    centre = field[1:-1, 1:-1]
    above = field[:-2, 1:-1]
    below = field[2:, 1:-1]
    leftside = field[1:-1, :-2]
    rightside = field[1:-1, 2:]
    result = centre + conx[:-2, 1:-1, None] * (above - centre)
    result = result + conx[1:-1, 1:-1, None] * (below - centre)
    result = result + cony[1:-1, :-2, None] * (leftside - centre)
    result = result + cony[1:-1, 1:-1, None] * (rightside - centre)
    return result


def per_device(adjoint, conduct_x, conduct_y, pick_weights, owner_order):
    cells_x, cells_y, total_cols = adjoint.shape
    picks = pick_weights.shape[0]
    full_x = cells_x * lax.axis_size("gx")
    full_y = cells_y * lax.axis_size("gy")
    rows_idx = lax.axis_index("gx") * cells_x + jnp.arange(cells_x, dtype=jnp.int32)[:, None]
    cols_idx = lax.axis_index("gy") * cells_y + jnp.arange(cells_y, dtype=jnp.int32)[None, :]
    conx = jnp.where(rows_idx < full_x - 1, conduct_x, jnp.float32(0.0))
    cony = jnp.where(cols_idx < full_y - 1, conduct_y, jnp.float32(0.0))
    stacked = jnp.stack([conx, cony])
    coeff_wide = extended(stacked, (("gx", 1), ("gy", 2)), STEPS)
    sorted_weights = jnp.take(pick_weights.reshape(picks, cells_x * cells_y), owner_order, axis=0)
    smooth_list = []
    repr_list = []
    for panel in range(PANELS):
        block = adjoint[:, :, panel * PANEL : (panel + 1) * PANEL]
        field = extended(block, (("gx", 0), ("gy", 1)), STEPS).astype(jnp.float32)
        coeffs = coeff_wide
        for step in range(STEPS):
            field = diffuse(field, coeffs[0], coeffs[1])
            coeffs = coeffs[:, 1:-1, 1:-1]
        rounded = field.astype(jnp.bfloat16)
        smooth_list.append(rounded)
        flat_panel = rounded.reshape(cells_x * cells_y, PANEL)
        owned = lax.psum_scatter(
            jnp.dot(sorted_weights, flat_panel, preferred_element_type=jnp.float32),
            ("gx", "gy"),
            scatter_dimension=0,
            tiled=True,
        )
        repr_list.append(owned)
    return (jnp.concatenate(smooth_list, axis=2), jnp.concatenate(repr_list, axis=1))


def solution(mesh):
    return jax.shard_map(
        per_device,
        mesh=mesh,
        in_specs=(P("gx", "gy", None), P("gx", "gy"), P("gx", "gy"), P(None, "gx", "gy"), P()),
        out_specs=(P("gx", "gy", None), P(("gx", "gy"), None)),
        check_vma=False,
    )
```

profile of v0, /device:TPU:0, one launch (start us, length us, event | category | flops | bytes accessed | tf_op | source)
XLA Modules:
  0.0 209.3 jit_solution(832288842762734524)
XLA Ops:
  7.3 0.9 select_bitcast_fusion
  8.2 2.4 %collective-permute-start.4 = (f32[2,4,128]{2,1,0:T(4,128)S(1)}, f32[2,4,128]{2,1,0:T(4,128)S(1)}, u32[]{:S(2)}, u32[]{:S(2)}) collective-permute-start(f32[2,4,128]{2,1,0:T(4,128)S(1)} %get-tuple-element.48), channel_id=1, source_target_pairs={{0,2},{2,4},{4,6},{6,8},{8,10},{10,12},{12,14},{14,16},{16,18},{18... | collective-permute-start | bytes 12296 | tf_op jit(solution)/shard_map/ppermute | solution.py:18
  10.6 1.4 collective-permute-start.5
  12.1 2.2 %fusion.70 = (bf16[4,128,256]{2,1,0:T(8,128)(2,1)}, bf16[4,128,256]{2,1,0:T(8,128)(2,1)}, bf16[4,128,256]{2,1,0:T(8,128)(2,1)}, bf16[4,128,256]{2,1,0:T(8,128)(2,1)}) fusion(bf16[16,128,512]{2,1,0:T(8,128)(2,1)} %param.5), kind=kLoop, calls=%fused_computation.136 | loop fusion | bytes 2097152 | tf_op jit(solution)/shard_map/slice | solution.py:16
  14.3 5.1 %collective-permute-start.8 = (bf16[4,128,256]{2,1,0:T(8,128)(2,1)}, bf16[4,128,256]{2,1,0:T(8,128)(2,1)S(1)}, u32[]{:S(2)}, u32[]{:S(2)}) collective-permute-start(bf16[4,128,256]{2,1,0:T(8,128)(2,1)} %get-tuple-element.5), channel_id=1, source_target_pairs={{0,2},{2,4},{4,6},{6,8},{8,10},{10,12},{12,14},{14,16},{16,18},{18... | collective-permute-start | bytes 786440 | tf_op jit(solution)/shard_map/ppermute | solution.py:18
  19.4 1.3 collective-permute-start.9
  20.7 4.3 %collective-permute-start = (bf16[4,128,256]{2,1,0:T(8,128)(2,1)}, bf16[4,128,256]{2,1,0:T(8,128)(2,1)S(1)}, u32[]{:S(2)}, u32[]{:S(2)}) collective-permute-start(bf16[4,128,256]{2,1,0:T(8,128)(2,1)} %get-tuple-element.4), channel_id=1, source_target_pairs={{0,2},{2,4},{4,6},{6,8},{8,10},{10,12},{12,14},{14,16},{16,18},{18... | collective-permute-start | bytes 786440 | tf_op jit(solution)/shard_map/ppermute | solution.py:18
  25.9 3.4 %collective-permute-start.6 = (f32[2,24,4]{2,1,0:T(8,128)S(1)}, f32[2,24,4]{2,1,0:T(8,128)S(1)}, u32[]{:S(2)}, u32[]{:S(2)}) collective-permute-start(f32[2,24,4]{2,1,0:T(8,128)S(1)} %get-tuple-element.46), channel_id=1, source_target_pairs={{0,1},{2,3},{4,5},{6,7},{8,9},{10,11},{12,13},{14,15},{16,17},{18,... | collective-permute-start | bytes 2312 | tf_op jit(solution)/shard_map/ppermute | solution.py:18
  29.3 1.3 collective-permute-start.7
  31.5 1.3 collective-permute-start.1
  32.8 2.3 %collective-permute-done.7 = f32[2,24,4]{2,1,0:T(8,128)S(1)} collective-permute-done((f32[2,24,4]{2,1,0:T(8,128)S(1)}, f32[2,24,4]{2,1,0:T(8,128)S(1)}, u32[]{:S(2)}, u32[]{:S(2)}) %collective-permute-start.7) | collective-permute-done | bytes 800 | tf_op jit(solution)/shard_map/ppermute | solution.py:19
  37.9 2.3 %collective-permute-start.10 = (bf16[24,4,256]{2,1,0:T(4,128)(2,1)S(1)}, bf16[24,4,256]{2,1,0:T(4,128)(2,1)S(1)}, u32[]{:S(2)}, u32[]{:S(2)}) collective-permute-start(bf16[24,4,256]{2,1,0:T(4,128)(2,1)S(1)} %get-tuple-element.12), channel_id=1, source_target_pairs={{0,1},{2,3},{4,5},{6,7},{8,9},{10,11},{12,13},{14,15},{16,17},{18,... | collective-permute-start | bytes 147464 | tf_op jit(solution)/shard_map/ppermute | solution.py:18
  40.2 1.3 collective-permute-start.11
  41.5 4.5 %collective-permute-start.2 = (bf16[24,4,256]{2,1,0:T(4,128)(2,1)S(1)}, bf16[24,4,256]{2,1,0:T(4,128)(2,1)S(1)}, u32[]{:S(2)}, u32[]{:S(2)}) collective-permute-start(bf16[24,4,256]{2,1,0:T(4,128)(2,1)S(1)} %get-tuple-element.10), channel_id=1, source_target_pairs={{0,1},{2,3},{4,5},{6,7},{8,9},{10,11},{12,13},{14,15},{16,17},{18,... | collective-permute-start | bytes 147464 | tf_op jit(solution)/shard_map/ppermute | solution.py:18
  46.1 1.3 collective-permute-start.3
  48.0 4.6 %collective-permute-done.3 = bf16[24,4,256]{2,1,0:T(4,128)(2,1)S(1)} collective-permute-done((bf16[24,4,256]{2,1,0:T(4,128)(2,1)S(1)}, bf16[24,4,256]{2,1,0:T(4,128)(2,1)S(1)}, u32[]{:S(2)}, u32[]{:S(2)}) %collective-permute-start.3) | collective-permute-done | bytes 49184 | tf_op jit(solution)/shard_map/ppermute | solution.py:19
  53.1 5.2 %fusion.9 = (f32[22,134,256]{2,1,0:T(8,128)S(1)}, f32[22,134,256]{2,1,0:T(8,128)S(1)}) fusion(f32[24,136,256]{2,1,0:T(8,128)S(1)} %maximum_convert_fusion, f32[22,134]{1,0:T(8,128)S(1)} %copy-done.2, f32[22,134]{1,0:T(8,128)S(1)} %get-tuple-element.44, f32[22,134]{1,0:T(8,128)S(1)} %get-tuple-element.43, f32[22,134]{1,0:T(8,128)S(1)} %get-tuple-element.42, ...), kind=kLoop, calls=%fused_computation.15 | loop fusion | flops 18112512 | bytes 36272192 | tf_op jit(solution)/shard_map/add | solution.py:33
  58.3 4.5 %fusion.25 = (f32[20,132,256]{2,1,0:T(8,128)S(1)}, f32[20,132,256]{2,1,0:T(8,128)S(1)}) fusion(f32[22,134,256]{2,1,0:T(8,128)S(1)} %get-tuple-element.18, f32[20,132]{1,0:T(8,128)S(1)} %get-tuple-element.41, f32[20,132]{1,0:T(8,128)S(1)} %get-tuple-element.40, f32[20,132]{1,0:T(8,128)S(1)} %get-tuple-element.39, f32[20,132]{1,0:T(8,128)S(1)} %get-tuple-element.38, ...), kind=kLoop, calls=%fused_computation.39 | loop fusion | flops 16220160 | bytes 32482560 | tf_op jit(solution)/shard_map/add | solution.py:33
  62.8 3.8 %fusion.41 = (f32[18,130,256]{2,1,0:T(8,128)S(1)}, f32[18,130,256]{2,1,0:T(8,128)S(1)}) fusion(f32[20,132,256]{2,1,0:T(8,128)S(1)} %get-tuple-element.16, f32[18,130]{1,0:T(8,128)S(1)} %get-tuple-element.37, f32[18,130]{1,0:T(8,128)S(1)} %get-tuple-element.36, f32[18,130]{1,0:T(8,128)S(1)} %get-tuple-element.35, f32[18,130]{1,0:T(8,128)S(1)} %get-tuple-element.34, ...), kind=kLoop, calls=%fused_computation.63 | loop fusion | flops 14376960 | bytes 28791360 | tf_op jit(solution)/shard_map/add | solution.py:33
  66.7 3.4 %fusion.59 = (bf16[16,128,256]{2,1,0:T(8,128)(2,1)S(1)}, bf16[16,128,256]{2,1,0:T(8,128)(2,1)S(1)}) fusion(f32[18,130,256]{2,1,0:T(8,128)S(1)} %get-tuple-element.14, f32[16,128]{1,0:T(8,128)S(1)} %copy-done.6, f32[16,128]{1,0:T(8,128)S(1)} %copy-done.5, f32[16,128]{1,0:T(8,128)S(1)} %copy-done.4, f32[16,128]{1,0:T(8,128)S(1)} %copy-done.3, ...), kind=kLoop, calls=%fused_computation.89 | loop fusion | flops 13631488 | bytes 23101440 | tf_op jit(solution)/shard_map/convert_element_type | solution.py:58
  70.1 1.0 fusion.66
  71.0 1.0 fusion.67
  72.0 1.5 pad_maximum_fusion
  73.5 126.9 %all-reduce.5.cloned.1.call-done = (f32[64,256]{1,0:T(8,128)}, f32[64,256]{1,0:T(8,128)}) async-done(((f32[64,256]{1,0:T(8,128)}, f32[64,256]{1,0:T(8,128)}), (f32[64,256]{1,0:T(8,128)}, f32[64,256]{1,0:T(8,128)})) %all-reduce.5.cloned.1.call-update) | async-done | bytes 131088
  (61 shorter events, 7.7 us)
Async XLA Ops:
  7.2 193.3 %all-reduce.5.cloned.1.call-start = ((), (), s32[]{:S(2)}) async-start(), calls=%async_computation | async-start | bytes 262144
  7.2 17.7 %copy-start = (bf16[16,128,512]{2,1,0:T(8,128)(2,1)S(1)}, bf16[16,128,512]{2,1,0:T(8,128)(2,1)}, u32[]{:S(2)}) copy-start(bf16[16,128,512]{2,1,0:T(8,128)(2,1)} %param.5) | copy-start | bytes 6291460
  8.2 17.6 %collective-permute-start.4 = (f32[2,4,128]{2,1,0:T(4,128)S(1)}, f32[2,4,128]{2,1,0:T(4,128)S(1)}, u32[]{:S(2)}, u32[]{:S(2)}) collective-permute-start(f32[2,4,128]{2,1,0:T(4,128)S(1)} %get-tuple-element.48), channel_id=1, source_target_pairs={{0,2},{2,4},{4,6},{6,8},{8,10},{10,12},{12,14},{14,16},{16,18},{18... | collective-permute-start | bytes 12296 | tf_op jit(solution)/shard_map/ppermute | solution.py:18
  10.6 14.6 %copy-start.8 = (s32[64]{0:T(128)S(1)}, s32[64]{0:T(128)}, u32[]{:S(2)}) copy-start(s32[64]{0:T(128)} %param.9) | copy-start | bytes 772
  10.6 20.0 %copy-start.1 = (bf16[64,16,128]{2,1,0:T(8,128)(2,1)S(1)}, bf16[64,16,128]{2,1,0:T(8,128)(2,1)}, u32[]{:S(2)}) copy-start(bf16[64,16,128]{2,1,0:T(8,128)(2,1)} %param.8) | copy-start | bytes 786436
  10.6 15.2 %collective-permute-start.5 = (f32[2,4,128]{2,1,0:T(4,128)S(1)}, f32[2,4,128]{2,1,0:T(4,128)S(1)}, u32[]{:S(2)}, u32[]{:S(2)}) collective-permute-start(f32[2,4,128]{2,1,0:T(4,128)S(1)} %get-tuple-element.49), channel_id=1, source_target_pairs={{2,0},{4,2},{6,4},{8,6},{10,8},{12,10},{14,12},{16,14},{18,16},{20... | collective-permute-start | bytes 12296 | tf_op jit(solution)/shard_map/ppermute | solution.py:19
  14.3 23.6 %collective-permute-start.8 = (bf16[4,128,256]{2,1,0:T(8,128)(2,1)}, bf16[4,128,256]{2,1,0:T(8,128)(2,1)S(1)}, u32[]{:S(2)}, u32[]{:S(2)}) collective-permute-start(bf16[4,128,256]{2,1,0:T(8,128)(2,1)} %get-tuple-element.5), channel_id=1, source_target_pairs={{0,2},{2,4},{4,6},{6,8},{8,10},{10,12},{12,14},{14,16},{16,18},{18... | collective-permute-start | bytes 786440 | tf_op jit(solution)/shard_map/ppermute | solution.py:18
  19.4 18.4 %collective-permute-start.9 = (bf16[4,128,256]{2,1,0:T(8,128)(2,1)}, bf16[4,128,256]{2,1,0:T(8,128)(2,1)S(1)}, u32[]{:S(2)}, u32[]{:S(2)}) collective-permute-start(bf16[4,128,256]{2,1,0:T(8,128)(2,1)} %get-tuple-element.7), channel_id=1, source_target_pairs={{2,0},{4,2},{6,4},{8,6},{10,8},{12,10},{14,12},{16,14},{18,16},{20... | collective-permute-start | bytes 786440 | tf_op jit(solution)/shard_map/ppermute | solution.py:19
  20.7 20.8 %collective-permute-start = (bf16[4,128,256]{2,1,0:T(8,128)(2,1)}, bf16[4,128,256]{2,1,0:T(8,128)(2,1)S(1)}, u32[]{:S(2)}, u32[]{:S(2)}) collective-permute-start(bf16[4,128,256]{2,1,0:T(8,128)(2,1)} %get-tuple-element.4), channel_id=1, source_target_pairs={{0,2},{2,4},{4,6},{6,8},{8,10},{10,12},{12,14},{14,16},{16,18},{18... | collective-permute-start | bytes 786440 | tf_op jit(solution)/shard_map/ppermute | solution.py:18
  25.9 5.6 %collective-permute-start.6 = (f32[2,24,4]{2,1,0:T(8,128)S(1)}, f32[2,24,4]{2,1,0:T(8,128)S(1)}, u32[]{:S(2)}, u32[]{:S(2)}) collective-permute-start(f32[2,24,4]{2,1,0:T(8,128)S(1)} %get-tuple-element.46), channel_id=1, source_target_pairs={{0,1},{2,3},{4,5},{6,7},{8,9},{10,11},{12,13},{14,15},{16,17},{18,... | collective-permute-start | bytes 2312 | tf_op jit(solution)/shard_map/ppermute | solution.py:18
  29.3 5.7 %collective-permute-start.7 = (f32[2,24,4]{2,1,0:T(8,128)S(1)}, f32[2,24,4]{2,1,0:T(8,128)S(1)}, u32[]{:S(2)}, u32[]{:S(2)}) collective-permute-start(f32[2,24,4]{2,1,0:T(8,128)S(1)} %get-tuple-element.47), channel_id=1, source_target_pairs={{1,0},{3,2},{5,4},{7,6},{9,8},{11,10},{13,12},{15,14},{17,16},{19,... | collective-permute-start | bytes 2312 | tf_op jit(solution)/shard_map/ppermute | solution.py:19
  31.5 10.0 %collective-permute-start.1 = (bf16[4,128,256]{2,1,0:T(8,128)(2,1)}, bf16[4,128,256]{2,1,0:T(8,128)(2,1)S(1)}, u32[]{:S(2)}, u32[]{:S(2)}) collective-permute-start(bf16[4,128,256]{2,1,0:T(8,128)(2,1)} %get-tuple-element.6), channel_id=1, source_target_pairs={{2,0},{4,2},{6,4},{8,6},{10,8},{12,10},{14,12},{16,14},{18,16},{20... | collective-permute-start | bytes 786440 | tf_op jit(solution)/shard_map/ppermute | solution.py:19
  37.9 9.5 %collective-permute-start.10 = (bf16[24,4,256]{2,1,0:T(4,128)(2,1)S(1)}, bf16[24,4,256]{2,1,0:T(4,128)(2,1)S(1)}, u32[]{:S(2)}, u32[]{:S(2)}) collective-permute-start(bf16[24,4,256]{2,1,0:T(4,128)(2,1)S(1)} %get-tuple-element.12), channel_id=1, source_target_pairs={{0,1},{2,3},{4,5},{6,7},{8,9},{10,11},{12,13},{14,15},{16,17},{18,... | collective-permute-start | bytes 147464 | tf_op jit(solution)/shard_map/ppermute | solution.py:18
  40.2 7.2 %collective-permute-start.11 = (bf16[24,4,256]{2,1,0:T(4,128)(2,1)S(1)}, bf16[24,4,256]{2,1,0:T(4,128)(2,1)S(1)}, u32[]{:S(2)}, u32[]{:S(2)}) collective-permute-start(bf16[24,4,256]{2,1,0:T(4,128)(2,1)S(1)} %get-tuple-element.13), channel_id=1, source_target_pairs={{1,0},{3,2},{5,4},{7,6},{9,8},{11,10},{13,12},{15,14},{17,16},{19,... | collective-permute-start | bytes 147464 | tf_op jit(solution)/shard_map/ppermute | solution.py:19
  41.5 6.4 %collective-permute-start.2 = (bf16[24,4,256]{2,1,0:T(4,128)(2,1)S(1)}, bf16[24,4,256]{2,1,0:T(4,128)(2,1)S(1)}, u32[]{:S(2)}, u32[]{:S(2)}) collective-permute-start(bf16[24,4,256]{2,1,0:T(4,128)(2,1)S(1)} %get-tuple-element.10), channel_id=1, source_target_pairs={{0,1},{2,3},{4,5},{6,7},{8,9},{10,11},{12,13},{14,15},{16,17},{18,... | collective-permute-start | bytes 147464 | tf_op jit(solution)/shard_map/ppermute | solution.py:18
  46.1 6.5 %collective-permute-start.3 = (bf16[24,4,256]{2,1,0:T(4,128)(2,1)S(1)}, bf16[24,4,256]{2,1,0:T(4,128)(2,1)S(1)}, u32[]{:S(2)}, u32[]{:S(2)}) collective-permute-start(bf16[24,4,256]{2,1,0:T(4,128)(2,1)S(1)} %get-tuple-element.11), channel_id=1, source_target_pairs={{1,0},{3,2},{5,4},{7,6},{9,8},{11,10},{13,12},{15,14},{17,16},{19,... | collective-permute-start | bytes 147464 | tf_op jit(solution)/shard_map/ppermute | solution.py:19
  48.0 5.2 %copy-start.2 = (f32[22,134]{1,0:T(8,128)S(1)}, f32[22,134]{1,0:T(8,128)}, u32[]{:S(2)}) copy-start(f32[22,134]{1,0:T(8,128)} %get-tuple-element.45) | copy-start | bytes 35380
  62.8 3.9 %copy-start.3 = (f32[16,128]{1,0:T(8,128)S(1)}, f32[16,128]{1,0:T(8,128)}, u32[]{:S(2)}) copy-start(f32[16,128]{1,0:T(8,128)} %get-tuple-element.30) | copy-start | bytes 24580
  62.8 3.9 %copy-start.4 = (f32[16,128]{1,0:T(8,128)S(1)}, f32[16,128]{1,0:T(8,128)}, u32[]{:S(2)}) copy-start(f32[16,128]{1,0:T(8,128)} %get-tuple-element.31) | copy-start | bytes 24580
  62.8 3.9 %copy-start.5 = (f32[16,128]{1,0:T(8,128)S(1)}, f32[16,128]{1,0:T(8,128)}, u32[]{:S(2)}) copy-start(f32[16,128]{1,0:T(8,128)} %get-tuple-element.32) | copy-start | bytes 24580
  62.8 3.9 %copy-start.6 = (f32[16,128]{1,0:T(8,128)S(1)}, f32[16,128]{1,0:T(8,128)}, u32[]{:S(2)}) copy-start(f32[16,128]{1,0:T(8,128)} %get-tuple-element.33) | copy-start | bytes 24580
  66.7 3.4 %copy-start.7 = (pred[64]{0:T(512)(128)(4,1)S(1)}, pred[64]{0:T(512)(128)(4,1)}, u32[]{:S(2)}) copy-start(pred[64]{0:T(512)(128)(4,1)} %compare_and_fusion) | copy-start | bytes 196
Sparse Core Ops, SparseCore 0:
  72.2 128.2 all-reduce.4
where the time goes:
time: 210 us; the launch traced here: 209 us
  waiting for transfers between devices  134 us (64%)
  starting transfers between devices  30 us (14%)
  other arithmetic  21.6 us (10%)
  between operations  14.5 us (7%)
  local copies, waits for them, and re-layouts  7.45 us (4%)
    unnamed x2, waiting for transfers between devices  127 us
    ppermute x6, starting transfers between devices, extended(): before = lax.ppermute(last, axis, up)  22.1 us
    add x3, other arithmetic, diffuse(): result = result + cony[1:-1, 1:-1, None] * (rightside - centre)  13.5 us
    ppermute x6, starting transfers between devices, extended(): after = lax.ppermute(leading, axis, down)  7.88 us
    ppermute x6, waiting for transfers between devices, extended(): after = lax.ppermute(leading, axis, down)  6.89 us
  transfers between devices with their start and end apart: 13, of which 3 were waited for; matrix products, arithmetic and copies ran while one was open for 4% of the time, Pallas kernels for 0%

commit v1 on v0

v1 whole, which is shorter than its diff:
```python
import functools

import jax
import jax.numpy as jnp
from jax import lax
from jax.experimental import pallas as pl
from jax.experimental.pallas import tpu as pltpu
from jax.sharding import PartitionSpec as P

STEPS = 4
LANES = 128
SUB = 8
MESH = pl.DeviceIdType.MESH
DIRS = ((0, 1), (0, -1), (1, 1), (1, -1), (-1, 1), (-1, -1), (1, 0), (-1, 0))
F32 = jnp.float32
BF16 = jnp.bfloat16


def dir_id(dx, dy):
    return DIRS.index((dx, dy))


def kernel(
    nx, ny, adj, kx_ref, ky_ref, w_ref, order_ref, out, rep,
    eb, yb, kn, kxb, kyb, u, w32, wt, ps, rbuf,
    load_sem, a_send, a_recv, k_send, k_recv, r_send, r_recv,
):
    cx, cy, cols = adj.shape
    groups = cols // LANES
    ex = cx + 2 * STEPS
    ey = cy + SUB
    picks = w_ref.shape[0]
    n = nx * ny
    tile = ps.shape[0] // n
    gx = lax.axis_index("gx")
    gy = lax.axis_index("gy")
    me = gx * ny + gy

    def dev(t):
        return (t // ny, lax.rem(t, ny))

    barrier = pltpu.get_barrier_semaphore()

    @pl.loop(1, n)
    def _(k):
        pl.semaphore_signal(
            barrier, inc=1, device_id=dev(lax.rem(me + k, n)), device_id_type=MESH
        )

    own = pltpu.make_async_copy(adj, eb.at[pl.ds(STEPS, cx)], load_sem)
    own.start()

    def present(dx, dy):
        ok = None
        for d, g, size in ((dx, gx, nx), (dy, gy, ny)):
            if d == 1:
                c = g < size - 1
            elif d == -1:
                c = g > 0
            else:
                continue
            ok = c if ok is None else jnp.logical_and(ok, c)
        return ok

    def region(sx, sy):
        rows = {-1: pl.ds(0, STEPS), 0: pl.ds(STEPS, cx), 1: pl.ds(STEPS + cx, STEPS)}[sx]
        if sy == 0:
            return eb.at[rows]
        return yb.at[0 if sy == 1 else 1, rows]

    def copies(dx, dy):
        sx, sy = -dx, -dy
        slot, mine = dir_id(sx, sy), dir_id(dx, dy)
        target = (gx + dx, gy + dy)
        src = adj
        if dx:
            src = src.at[pl.ds(cx - STEPS if dx == 1 else 0, STEPS)]
        if dy:
            src = src.at[:, pl.ds(cy - SUB if dy == 1 else 0, SUB)]
        dst = region(sx, sy)
        result = []
        for a, kref in enumerate((kx_ref, ky_ref)):
            result.append(
                pltpu.make_async_remote_copy(
                    src_ref=kref, dst_ref=kn.at[slot, a], send_sem=k_send.at[mine, a],
                    recv_sem=k_recv.at[slot, a], device_id=target, device_id_type=MESH,
                )
            )
        parts = [(src, dst)]
        if dy == 0:
            parts = [
                (src.at[:, :, pl.ds(q * LANES, LANES)], dst.at[:, :, pl.ds(q * LANES, LANES)])
                for q in range(groups)
            ]
        for q, (s, d) in enumerate(parts):
            result.append(
                pltpu.make_async_remote_copy(
                    src_ref=s, dst_ref=d, send_sem=a_send.at[mine, q],
                    recv_sem=a_recv.at[slot, q], device_id=target, device_id_type=MESH,
                )
            )
        return result

    pick_ids = lax.broadcasted_iota(jnp.int32, (picks, picks), 0)
    chosen = jnp.where(pick_ids == order_ref[...], F32(1), F32(0)).astype(BF16)
    w32[...] = w_ref[...].astype(F32).reshape(picks * cx, LANES)

    def sort_weights():
        for x in range(cx):
            row = w32[pl.ds(x, picks, stride=cx), :].astype(BF16)
            row = lax.dot_general(
                chosen, row, (((0,), (0,)), ((), ())), preferred_element_type=F32
            )
            wt[:, x * LANES : (x + 1) * LANES] = row.astype(BF16)

    pl.semaphore_wait(barrier, n - 1)

    for dx, dy in DIRS:
        @pl.when(present(dx, dy))
        def _(dx=dx, dy=dy):
            for c in copies(dx, dy):
                c.start()

        @pl.when(jnp.logical_not(present(dx, dy)))
        def _(dx=dx, dy=dy):
            part = region(dx, dy)
            part[...] = jnp.zeros(part.shape, BF16)
            kn[dir_id(dx, dy)] = jnp.zeros(kn.shape[1:], F32)

    sort_weights()

    def wait_recv(dx, dy, what):
        @pl.when(present(dx, dy))
        def _():
            slot = dir_id(dx, dy)
            if what == "k":
                for a in range(2):
                    pltpu.make_async_copy(kn.at[slot, a], kn.at[slot, a], k_recv.at[slot, a]).wait()
            elif what == "a":
                part = region(dx, dy)
                pltpu.make_async_copy(part, part, a_recv.at[slot, 0]).wait()
            else:
                part = region(dx, dy).at[:, :, pl.ds(what * LANES, LANES)]
                pltpu.make_async_copy(part, part, a_recv.at[slot, what]).wait()

    for d in DIRS:
        wait_recv(*d, "k")

    low = lax.broadcasted_iota(jnp.int32, (SUB, cx), 0) < STEPS
    place = lax.broadcasted_iota(jnp.int32, (ey, cx), 0)
    for a, (kref, store) in enumerate(((kx_ref, kxb), (ky_ref, kyb))):
        for sx in (-1, 0, 1):
            def block(sy):
                if sx == 0 and sy == 0:
                    return kref[...]
                return kn[dir_id(sx, sy), a]

            main = block(0).T
            tail = jnp.where(low, block(1).T[:SUB], block(-1).T[cy - SUB :])
            whole = jnp.concatenate([main, tail], axis=0)
            if a == 1:
                whole = jnp.where(
                    jnp.logical_and(place == cy - 1, gy == ny - 1), F32(0), whole
                )
            rows = {-1: range(cx - STEPS, cx), 0: range(cx), 1: range(STEPS)}[sx]
            base = {-1: 0, 0: STEPS, 1: STEPS + cx}[sx]
            for i, r in enumerate(rows):
                column = jnp.broadcast_to(whole[:, r : r + 1], (ey, LANES))
                if a == 0 and sx == 0 and r == cx - 1:
                    column = jnp.where(gx == nx - 1, F32(0), column)
                store[base + i] = column

    low_lane = lax.broadcasted_iota(jnp.int32, (SUB, LANES), 0) < STEPS

    def lanes(q):
        if isinstance(q, int):
            return pl.ds(q * LANES, LANES)
        return pl.ds(pl.multiple_of(q * LANES, LANES), LANES)

    def assemble(q, lo, hi):
        @pl.loop(lo, hi)
        def _(e):
            u[0, q, e, :cy] = eb[e, :, lanes(q)].astype(F32)
            right = yb[0, e, :, lanes(q)].astype(F32)
            left = yb[1, e, :, lanes(q)].astype(F32)
            u[0, q, e, cy:] = jnp.where(low_lane, right, left)

    def sweep(level, q, lo, hi):
        here = u[level, q, lo]
        before = kxb[lo - 1] * (here - u[level, q, lo - 1])

        def body(e, carry):
            here, before = carry
            below = u[level, q, e + 1]
            after = kxb[e] * (below - here)
            side = kyb[e] * (pltpu.roll(here, ey - 1, 0) - here)
            value = (here + (after - before)) + (side - pltpu.roll(side, 1, 0))
            if level < STEPS - 1:
                u[level + 1, q, e] = value
            else:
                out[e - STEPS, :, lanes(q)] = value[:cy].astype(BF16)
            return below, after

        lax.fori_loop(lo, hi, body, (here, before))

    def product(lo, hi):
        return jnp.dot(
            wt[:, lo * LANES : hi * LANES],
            out[lo:hi].reshape((hi - lo) * cy, cols),
            preferred_element_type=F32,
        )

    own.wait()
    for d in DIRS[:2]:
        wait_recv(*d, "a")

    @pl.loop(0, groups)
    def _(q):
        assemble(q, STEPS, STEPS + cx)
        for s in range(1, STEPS + 1):
            sweep(s - 1, q, STEPS + s, STEPS + cx - s)

    for d in DIRS[2:6]:
        wait_recv(*d, "a")
    for q in range(groups):
        for d in DIRS[6:]:
            wait_recv(*d, q)
        assemble(q, 0, STEPS)
        assemble(q, STEPS + cx, ex)
        for s in range(1, STEPS + 1):
            sweep(s - 1, q, s, STEPS + s)
            sweep(s - 1, q, STEPS + cx - s, ex - s)

    total = product(0, cx)
    for q in range(groups):
        ps[pl.ds(q, picks, stride=groups), :] = total[:, q * LANES : (q + 1) * LANES]

    def reduce_copy(k):
        t = lax.rem(me + k, n)
        return pltpu.make_async_remote_copy(
            src_ref=ps.at[pl.ds(pl.multiple_of(t * tile, tile), tile)],
            dst_ref=rbuf.at[k - 1], send_sem=r_send.at[k - 1], recv_sem=r_recv.at[k - 1],
            device_id=dev(t), device_id_type=MESH,
        )

    @pl.loop(1, n)
    def _(k):
        reduce_copy(k).start()

    for dx, dy in DIRS:
        @pl.when(present(dx, dy))
        def _(dx=dx, dy=dy):
            for c in copies(dx, dy):
                c.wait_send()

    @pl.loop(1, n)
    def _(k):
        reduce_copy(k).wait()

    total = ps[pl.ds(pl.multiple_of(me * tile, tile), tile), :]
    total = total + jnp.sum(rbuf[...], axis=0)
    for r in range(tile // groups):
        for q in range(groups):
            rep[r : r + 1, q * LANES : (q + 1) * LANES] = total[
                r * groups + q : r * groups + q + 1
            ]


def solution(mesh):
    nx, ny = mesh.shape["gx"], mesh.shape["gy"]
    n = nx * ny

    def per_device(adjoint, conduct_x, conduct_y, pick_weights, owner_order):
        cx, cy, cols = adjoint.shape
        picks = pick_weights.shape[0]
        groups = cols // LANES
        ex, ey = cx + 2 * STEPS, cy + SUB
        tile = picks // n * groups
        vmem = pl.BlockSpec(memory_space=pltpu.VMEM)
        dma = pltpu.SemaphoreType.DMA
        return pl.pallas_call(
            functools.partial(kernel, nx, ny),
            out_shape=(
                jax.ShapeDtypeStruct((cx, cy, cols), BF16),
                jax.ShapeDtypeStruct((picks // n, cols), F32),
            ),
            in_specs=[pl.BlockSpec(memory_space=pl.ANY)] + [vmem] * 4,
            out_specs=(vmem, vmem),
            scratch_shapes=[
                pltpu.VMEM((ex, cy, cols), BF16),
                pltpu.VMEM((2, ex, SUB, cols), BF16),
                pltpu.VMEM((len(DIRS), 2, cx, cy), F32),
                pltpu.VMEM((ex, ey, LANES), F32),
                pltpu.VMEM((ex, ey, LANES), F32),
                pltpu.VMEM((STEPS, groups, ex, ey, LANES), F32),
                pltpu.VMEM((picks * cx, LANES), F32),
                pltpu.VMEM((picks, cx * cy), BF16),
                pltpu.VMEM((picks * groups, LANES), F32),
                pltpu.VMEM((n - 1, tile, LANES), F32),
                dma,
                dma((len(DIRS), groups)),
                dma((len(DIRS), groups)),
                dma((len(DIRS), 2)),
                dma((len(DIRS), 2)),
                dma((n - 1,)),
                dma((n - 1,)),
            ],
            compiler_params=pltpu.CompilerParams(
                collective_id=0, has_side_effects=True, vmem_limit_bytes=56 << 20
            ),
        )(adjoint, conduct_x, conduct_y, pick_weights, owner_order.reshape(1, picks))

    return jax.shard_map(
        per_device,
        mesh=mesh,
        in_specs=(P("gx", "gy", None), P("gx", "gy"), P("gx", "gy"), P(None, "gx", "gy"), P()),
        out_specs=(P("gx", "gy", None), P(("gx", "gy"), None)),
        check_vma=False,
    )
```

time: 210 us -> 41.4 us (0.20)
  waiting for transfers between devices: 134 us -> 0 us
  Pallas kernels: 0 us -> 36.8 us
  starting transfers between devices: 30 us -> 0 us
  other arithmetic: 21.6 us -> 0 us
  between operations: 14.5 us -> 0.65 us
  local copies, waits for them, and re-layouts: 7.45 us -> 3.69 us
    unnamed x2 -> x0, waiting for transfers between devices: 127 us -> none
    pallas_call x0 -> x1, Pallas kernels: none -> 36.8 us  [per_device(): pl.pallas_call(functools.partial(kernel, nx, ny), out_shape=(jax.ShapeDty...]
    ppermute x12 -> x0, starting transfers between devices: 29.9 us -> none  [the longest x6 22.1 us: extended(): before = lax.ppermute(last, axis, up)]
    add x3 -> x0, other arithmetic: 13.5 us -> none  [diffuse(): result = result + cony[1:-1, 1:-1, None] * (rightside - centre)]
    ppermute x12 -> x0, waiting for transfers between devices: 6.9 us -> none  [the longest x6 6.89 us: extended(): after = lax.ppermute(leading, axis, down)]
    slice x11 -> x0, local copies, waits for them, and re-layouts: 4.94 us -> none  [the longest x2 2.26 us: extended(): last = lax.slice_in_dim(array, length - width, length, axis=dim)]
    convert_element_type x3 -> x0, other arithmetic: 4.4 us -> none  [the longest x1 3.35 us: per_device(): rounded = field.astype(jnp.bfloat16)]
    concatenate x4 -> x0, other arithmetic: 2.21 us -> none  [the longest x1 1.5 us: per_device(): jnp.concatenate(smooth_list, axis=2)]
  transfers between devices with their start and end apart: 13 -> 0, of which waited for: 3 -> 0; matrix products, arithmetic and copies ran while one was open for 4% -> 0% of each run, Pallas kernels for 0% -> 0%
where the time goes in v1:
time: 41.4 us; the launch traced here: 41.2 us
  Pallas kernels  36.8 us (89%)
  local copies, waits for them, and re-layouts  3.69 us (9%)
  between operations  0.65 us (2%)
    pallas_call x1, Pallas kernels, per_device(): pl.pallas_call(functools.partial(kernel, nx, ny), out_shape=(jax.ShapeDty...  36.8 us
    unnamed x4, local copies, waits for them, and re-layouts  3.69 us

profile of v1, /device:TPU:0, one launch (start us, length us, event | category | flops | bytes accessed | tf_op | source)
XLA Modules:
  0.0 41.2 jit_solution(4397925184044984089)
XLA Ops:
  0.6 36.8 %shard_map.68 = (bf16[16,128,512]{2,1,0:T(8,128)(2,1)}, f32[2,512]{1,0:T(2,128)}) custom-call(bf16[16,128,512]{2,1,0:T(8,128)(2,1)} %adj.1, f32[16,128]{1,0:T(8,128)} %kx_ref.1, f32[16,128]{1,0:T(8,128)} %ky_ref.1, bf16[64,16,128]{2,1,0:T(8,128)(2,1)} %w_ref.1, s32[1,64]{1,0:T(1,128)} %bitcast.1), custom_call_target="tpu_custom_call" | custom-call | tf_op jit(solution)/shard_map/pallas_call | solution.py:281
  37.5 0.0 copy-start
  37.5 3.1 %copy.9 = bf16[16,128,512]{2,1,0:T(8,128)(2,1)} copy(bf16[16,128,512]{2,1,0:T(8,128)(2,1)} %get-tuple-element.4) | data formatting | bytes 4194304
  40.6 0.0 copy-done
  40.6 0.6 %copy.10 = f32[2,512]{1,0:T(2,128)} copy(f32[2,512]{1,0:T(2,128)S(1)} %copy-done) | data formatting | bytes 8192
Async XLA Ops:
  37.5 3.1 %copy-start = (f32[2,512]{1,0:T(2,128)S(1)}, f32[2,512]{1,0:T(2,128)}, u32[]{:S(2)}) copy-start(f32[2,512]{1,0:T(2,128)} %get-tuple-element.5) | copy-start | bytes 12292

commit v2 on v1

--- a/solution.py
+++ b/solution.py
@@ -21,9 +21,9 @@
 
 
 def kernel(
-    nx, ny, adj, kx_ref, ky_ref, w_ref, order_ref, out, rep,
-    eb, yb, kn, kxb, kyb, u, w32, wt, ps, rbuf,
-    load_sem, a_send, a_recv, k_send, k_recv, r_send, r_recv,
+    nx, ny, adj, kx_ref, ky_ref, w_ref, order_ref, out_hbm, rep,
+    out, eb, yb, kn, kxb, kyb, u, w32, wt, ps, rbuf,
+    load_sem, out_sem, a_send, a_recv, k_send, k_recv, r_send, r_recv,
 ):
     cx, cy, cols = adj.shape
     groups = cols // LANES
@@ -113,6 +113,23 @@
             )
             wt[:, x * LANES : (x + 1) * LANES] = row.astype(BF16)
 
+    def lanes(q):
+        if isinstance(q, int):
+            return pl.ds(q * LANES, LANES)
+        return pl.ds(pl.multiple_of(q * LANES, LANES), LANES)
+
+    def widen(q, lo, hi):
+        @pl.loop(lo, hi)
+        def _(e):
+            u[0, q, e, :cy] = eb[e, :, lanes(q)].astype(F32)
+
+    sort_weights()
+    own.wait()
+
+    @pl.loop(0, groups)
+    def _(q):
+        widen(q, STEPS, STEPS + cx)
+
     pl.semaphore_wait(barrier, n - 1)
 
     for dx, dy in DIRS:
@@ -126,8 +143,6 @@
             part = region(dx, dy)
             part[...] = jnp.zeros(part.shape, BF16)
             kn[dir_id(dx, dy)] = jnp.zeros(kn.shape[1:], F32)
-
-    sort_weights()
 
     def wait_recv(dx, dy, what):
         @pl.when(present(dx, dy))
@@ -172,15 +187,9 @@
 
     low_lane = lax.broadcasted_iota(jnp.int32, (SUB, LANES), 0) < STEPS
 
-    def lanes(q):
-        if isinstance(q, int):
-            return pl.ds(q * LANES, LANES)
-        return pl.ds(pl.multiple_of(q * LANES, LANES), LANES)
-
-    def assemble(q, lo, hi):
+    def fringe(q, lo, hi):
         @pl.loop(lo, hi)
         def _(e):
-            u[0, q, e, :cy] = eb[e, :, lanes(q)].astype(F32)
             right = yb[0, e, :, lanes(q)].astype(F32)
             left = yb[1, e, :, lanes(q)].astype(F32)
             u[0, q, e, cy:] = jnp.where(low_lane, right, left)
@@ -210,13 +219,12 @@
             preferred_element_type=F32,
         )
 
-    own.wait()
     for d in DIRS[:2]:
         wait_recv(*d, "a")
 
     @pl.loop(0, groups)
     def _(q):
-        assemble(q, STEPS, STEPS + cx)
+        fringe(q, STEPS, STEPS + cx)
         for s in range(1, STEPS + 1):
             sweep(s - 1, q, STEPS + s, STEPS + cx - s)
 
@@ -225,12 +233,15 @@
     for q in range(groups):
         for d in DIRS[6:]:
             wait_recv(*d, q)
-        assemble(q, 0, STEPS)
-        assemble(q, STEPS + cx, ex)
+        for lo in (0, STEPS + cx):
+            widen(q, lo, lo + STEPS)
+            fringe(q, lo, lo + STEPS)
         for s in range(1, STEPS + 1):
             sweep(s - 1, q, s, STEPS + s)
             sweep(s - 1, q, STEPS + cx - s, ex - s)
 
+    store = pltpu.make_async_copy(out, out_hbm, out_sem)
+    store.start()
     total = product(0, cx)
     for q in range(groups):
         ps[pl.ds(q, picks, stride=groups), :] = total[:, q * LANES : (q + 1) * LANES]
@@ -264,6 +275,28 @@
             rep[r : r + 1, q * LANES : (q + 1) * LANES] = total[
                 r * groups + q : r * groups + q + 1
             ]
+    store.wait()
+
+
+def copy_kernel(src, small, dst, small_dst, buf, sem_in, sem_out):
+    small_dst[...] = small[...]
+    parts = buf.shape[0]
+    rows = src.shape[0] // parts
+
+    def moves(i):
+        own = pl.ds(i * rows, rows)
+        return (
+            pltpu.make_async_copy(src.at[own], buf.at[i], sem_in.at[i]),
+            pltpu.make_async_copy(buf.at[i], dst.at[own], sem_out.at[i]),
+        )
+
+    for i in range(parts):
+        moves(i)[0].start()
+    for i in range(parts):
+        moves(i)[0].wait()
+        moves(i)[1].start()
+    for i in range(parts):
+        moves(i)[1].wait()
 
 
 def solution(mesh):
@@ -278,15 +311,17 @@
         tile = picks // n * groups
         vmem = pl.BlockSpec(memory_space=pltpu.VMEM)
         dma = pltpu.SemaphoreType.DMA
-        return pl.pallas_call(
+        any_space = pl.BlockSpec(memory_space=pl.ANY)
+        smoothed, owned = pl.pallas_call(
             functools.partial(kernel, nx, ny),
             out_shape=(
                 jax.ShapeDtypeStruct((cx, cy, cols), BF16),
                 jax.ShapeDtypeStruct((picks // n, cols), F32),
             ),
-            in_specs=[pl.BlockSpec(memory_space=pl.ANY)] + [vmem] * 4,
-            out_specs=(vmem, vmem),
+            in_specs=[any_space] + [vmem] * 4,
+            out_specs=(any_space, vmem),
             scratch_shapes=[
+                pltpu.VMEM((cx, cy, cols), BF16),
                 pltpu.VMEM((ex, cy, cols), BF16),
                 pltpu.VMEM((2, ex, SUB, cols), BF16),
                 pltpu.VMEM((len(DIRS), 2, cx, cy), F32),
@@ -297,6 +332,7 @@
                 pltpu.VMEM((picks, cx * cy), BF16),
                 pltpu.VMEM((picks * groups, LANES), F32),
                 pltpu.VMEM((n - 1, tile, LANES), F32),
+                dma,
                 dma,
                 dma((len(DIRS), groups)),
                 dma((len(DIRS), groups)),
@@ -309,6 +345,21 @@
                 collective_id=0, has_side_effects=True, vmem_limit_bytes=56 << 20
             ),
         )(adjoint, conduct_x, conduct_y, pick_weights, owner_order.reshape(1, picks))
+        parts = 4
+        return pl.pallas_call(
+            copy_kernel,
+            out_shape=(
+                jax.ShapeDtypeStruct((cx, cy, cols), BF16),
+                jax.ShapeDtypeStruct((picks // n, cols), F32),
+            ),
+            in_specs=[any_space, vmem],
+            out_specs=(any_space, vmem),
+            scratch_shapes=[
+                pltpu.VMEM((parts, cx // parts, cy, cols), BF16),
+                dma((parts,)),
+                dma((parts,)),
+            ],
+        )(smoothed, owned)
 
     return jax.shard_map(
         per_device,

time: 41.4 us -> 40.7 us (0.983)
  local copies, waits for them, and re-layouts: 3.69 us -> 0 us
  Pallas kernels: 36.8 us -> 39.9 us
    unnamed x4 -> x0, local copies, waits for them, and re-layouts: 3.69 us -> none
    pallas_call x0 -> x1, Pallas kernels: none -> 3.69 us  [per_device(): pl.pallas_call(copy_kernel, out_shape=(jax.ShapeDtypeStruct((cx, cy, cols...]
    pallas_call x1, Pallas kernels: 36.8 us -> 36.2 us  [per_device(): pl.pallas_call(functools.partial(kernel, nx, ny), out_shape=(jax.ShapeDty...]
where the time goes in v2:
time: 40.7 us; the launch traced here: 40.5 us
  Pallas kernels  39.9 us (98%)
  between operations  0.64 us (2%)
    pallas_call x1, Pallas kernels, per_device(): pl.pallas_call(functools.partial(kernel, nx, ny), out_shape=(jax.ShapeDty...  36.2 us
    pallas_call x1, Pallas kernels, per_device(): pl.pallas_call(copy_kernel, out_shape=(jax.ShapeDtypeStruct((cx, cy, cols...  3.69 us

profile of v2, /device:TPU:0, one launch (start us, length us, event | category | flops | bytes accessed | tf_op | source)
XLA Modules:
  0.0 40.5 jit_solution(8789583233504139916)
XLA Ops:
  0.6 36.2 %shard_map.68 = (bf16[16,128,512]{2,1,0:T(8,128)(2,1)}, f32[2,512]{1,0:T(2,128)}) custom-call(bf16[16,128,512]{2,1,0:T(8,128)(2,1)} %adj.1, f32[16,128]{1,0:T(8,128)} %kx_ref.1, f32[16,128]{1,0:T(8,128)} %ky_ref.1, bf16[64,16,128]{2,1,0:T(8,128)(2,1)} %w_ref.1, s32[1,64]{1,0:T(1,128)} %bitcast.1), custom_call_target="tpu_custom_call" | custom-call | tf_op jit(solution)/shard_map/pallas_call | solution.py:315
  36.8 3.7 %shard_map.69 = (bf16[16,128,512]{2,1,0:T(8,128)(2,1)}, f32[2,512]{1,0:T(2,128)}) custom-call(bf16[16,128,512]{2,1,0:T(8,128)(2,1)} %get-tuple-element.4.src, f32[2,512]{1,0:T(2,128)} %get-tuple-element.5.small), custom_call_target="tpu_custom_call" | custom-call | tf_op jit(solution)/shard_map/pallas_call | solution.py:349

commit v3 on v2

--- a/solution.py
+++ b/solution.py
@@ -123,7 +123,23 @@
         def _(e):
             u[0, q, e, :cy] = eb[e, :, lanes(q)].astype(F32)
 
-    sort_weights()
+    place = lax.broadcasted_iota(jnp.int32, (cy, cx), 0)
+
+    def own_k(a, block):
+        main = block.T
+        if a == 1:
+            edge = jnp.logical_and(place == cy - 1, gy == ny - 1)
+            main = jnp.where(edge, F32(0), main)
+        return main
+
+    for a, (kref, kstore) in enumerate(((kx_ref, kxb), (ky_ref, kyb))):
+        main = own_k(a, kref[...])
+        for r in range(cx):
+            column = jnp.broadcast_to(main[:, r : r + 1], (cy, LANES))
+            if a == 0 and r == cx - 1:
+                column = jnp.where(gx == nx - 1, F32(0), column)
+            kstore[STEPS + r, :cy] = column
+
     own.wait()
 
     @pl.loop(0, groups)
@@ -158,33 +174,6 @@
                 part = region(dx, dy).at[:, :, pl.ds(what * LANES, LANES)]
                 pltpu.make_async_copy(part, part, a_recv.at[slot, what]).wait()
 
-    for d in DIRS:
-        wait_recv(*d, "k")
-
-    low = lax.broadcasted_iota(jnp.int32, (SUB, cx), 0) < STEPS
-    place = lax.broadcasted_iota(jnp.int32, (ey, cx), 0)
-    for a, (kref, store) in enumerate(((kx_ref, kxb), (ky_ref, kyb))):
-        for sx in (-1, 0, 1):
-            def block(sy):
-                if sx == 0 and sy == 0:
-                    return kref[...]
-                return kn[dir_id(sx, sy), a]
-
-            main = block(0).T
-            tail = jnp.where(low, block(1).T[:SUB], block(-1).T[cy - SUB :])
-            whole = jnp.concatenate([main, tail], axis=0)
-            if a == 1:
-                whole = jnp.where(
-                    jnp.logical_and(place == cy - 1, gy == ny - 1), F32(0), whole
-                )
-            rows = {-1: range(cx - STEPS, cx), 0: range(cx), 1: range(STEPS)}[sx]
-            base = {-1: 0, 0: STEPS, 1: STEPS + cx}[sx]
-            for i, r in enumerate(rows):
-                column = jnp.broadcast_to(whole[:, r : r + 1], (ey, LANES))
-                if a == 0 and sx == 0 and r == cx - 1:
-                    column = jnp.where(gx == nx - 1, F32(0), column)
-                store[base + i] = column
-
     low_lane = lax.broadcasted_iota(jnp.int32, (SUB, LANES), 0) < STEPS
 
     def fringe(q, lo, hi):
@@ -194,18 +183,19 @@
             left = yb[1, e, :, lanes(q)].astype(F32)
             u[0, q, e, cy:] = jnp.where(low_lane, right, left)
 
-    def sweep(level, q, lo, hi):
-        here = u[level, q, lo]
-        before = kxb[lo - 1] * (here - u[level, q, lo - 1])
+    def sweep(level, q, lo, hi, wide=ey):
+        own_cols = pl.ds(0, wide)
+        here = u[level, q, lo, own_cols]
+        before = kxb[lo - 1, own_cols] * (here - u[level, q, lo - 1, own_cols])
 
         def body(e, carry):
             here, before = carry
-            below = u[level, q, e + 1]
-            after = kxb[e] * (below - here)
-            side = kyb[e] * (pltpu.roll(here, ey - 1, 0) - here)
+            below = u[level, q, e + 1, own_cols]
+            after = kxb[e, own_cols] * (below - here)
+            side = kyb[e, own_cols] * (pltpu.roll(here, wide - 1, 0) - here)
             value = (here + (after - before)) + (side - pltpu.roll(side, 1, 0))
             if level < STEPS - 1:
-                u[level + 1, q, e] = value
+                u[level + 1, q, e, own_cols] = value
             else:
                 out[e - STEPS, :, lanes(q)] = value[:cy].astype(BF16)
             return below, after
@@ -219,14 +209,81 @@
             preferred_element_type=F32,
         )
 
+    @pl.loop(0, groups)
+    def _(q):
+        for s in range(1, STEPS + 1):
+            sweep(s - 1, q, STEPS + s, STEPS + cx - s, cy)
+
+    sort_weights()
+
+    for d in DIRS:
+        wait_recv(*d, "k")
+
+    low = lax.broadcasted_iota(jnp.int32, (SUB, cx), 0) < STEPS
+    for a, store in enumerate((kxb, kyb)):
+        for sx in (-1, 0, 1):
+            tail = jnp.where(
+                low,
+                kn[dir_id(sx, 1), a].T[:SUB],
+                kn[dir_id(sx, -1), a].T[cy - SUB :],
+            )
+            main = None if sx == 0 else own_k(a, kn[dir_id(sx, 0), a])
+            rows = {-1: range(cx - STEPS, cx), 0: range(cx), 1: range(STEPS)}[sx]
+            base = {-1: 0, 0: STEPS, 1: STEPS + cx}[sx]
+            for i, r in enumerate(rows):
+                column = jnp.broadcast_to(tail[:, r : r + 1], (SUB, LANES))
+                if a == 0 and sx == 0 and r == cx - 1:
+                    column = jnp.where(gx == nx - 1, F32(0), column)
+                store[base + i, cy:] = column
+                if sx:
+                    store[base + i, :cy] = jnp.broadcast_to(main[:, r : r + 1], (cy, LANES))
+
     for d in DIRS[:2]:
         wait_recv(*d, "a")
 
     @pl.loop(0, groups)
     def _(q):
         fringe(q, STEPS, STEPS + cx)
-        for s in range(1, STEPS + 1):
-            sweep(s - 1, q, STEPS + s, STEPS + cx - s)
+
+    def strips(level, lo, hi):
+        span = 3 * SUB
+
+        def window(get):
+            return jnp.concatenate(
+                [get(pl.ds(cy - SUB, 2 * SUB)), get(pl.ds(0, SUB))], axis=0
+            )
+
+        @pl.loop(lo, hi)
+        def _(e):
+            up = window(lambda c: kxb[e - 1, c])
+            down = window(lambda c: kxb[e, c])
+            along = window(lambda c: kyb[e, c])
+            for q in range(groups):
+                here = window(lambda c: u[level, q, e, c])
+                above = window(lambda c: u[level, q, e - 1, c])
+                below = window(lambda c: u[level, q, e + 1, c])
+                flow = down * (below - here) - up * (here - above)
+                side = along * (pltpu.roll(here, span - 1, 0) - here)
+                value = (here + flow) + (side - pltpu.roll(side, 1, 0))
+                first, mid, last = (value[i * SUB : (i + 1) * SUB] for i in range(3))
+                if level < STEPS - 1:
+                    head = u[level + 1, q, e, cy - SUB : cy]
+                    foot = u[level + 1, q, e, :SUB]
+                    u[level + 1, q, e, cy - SUB : cy] = jnp.where(low_lane, head, first)
+                    u[level + 1, q, e, cy:] = mid
+                    u[level + 1, q, e, :SUB] = jnp.where(low_lane, last, foot)
+                else:
+                    head = out[e - STEPS, cy - SUB :, lanes(q)].astype(F32)
+                    foot = out[e - STEPS, :SUB, lanes(q)].astype(F32)
+                    out[e - STEPS, cy - SUB :, lanes(q)] = jnp.where(
+                        low_lane, head, first
+                    ).astype(BF16)
+                    out[e - STEPS, :SUB, lanes(q)] = jnp.where(
+                        low_lane, last, foot
+                    ).astype(BF16)
+
+    for s in range(1, STEPS + 1):
+        strips(s - 1, STEPS + s, STEPS + cx - s)
 
     for d in DIRS[2:6]:
         wait_recv(*d, "a")
@@ -276,27 +333,6 @@
                 r * groups + q : r * groups + q + 1
             ]
     store.wait()
-
-
-def copy_kernel(src, small, dst, small_dst, buf, sem_in, sem_out):
-    small_dst[...] = small[...]
-    parts = buf.shape[0]
-    rows = src.shape[0] // parts
-
-    def moves(i):
-        own = pl.ds(i * rows, rows)
-        return (
-            pltpu.make_async_copy(src.at[own], buf.at[i], sem_in.at[i]),
-            pltpu.make_async_copy(buf.at[i], dst.at[own], sem_out.at[i]),
-        )
-
-    for i in range(parts):
-        moves(i)[0].start()
-    for i in range(parts):
-        moves(i)[0].wait()
-        moves(i)[1].start()
-    for i in range(parts):
-        moves(i)[1].wait()
 
 
 def solution(mesh):
@@ -345,21 +381,7 @@
                 collective_id=0, has_side_effects=True, vmem_limit_bytes=56 << 20
             ),
         )(adjoint, conduct_x, conduct_y, pick_weights, owner_order.reshape(1, picks))
-        parts = 4
-        return pl.pallas_call(
-            copy_kernel,
-            out_shape=(
-                jax.ShapeDtypeStruct((cx, cy, cols), BF16),
-                jax.ShapeDtypeStruct((picks // n, cols), F32),
-            ),
-            in_specs=[any_space, vmem],
-            out_specs=(any_space, vmem),
-            scratch_shapes=[
-                pltpu.VMEM((parts, cx // parts, cy, cols), BF16),
-                dma((parts,)),
-                dma((parts,)),
-            ],
-        )(smoothed, owned)
+        return smoothed, owned
 
     return jax.shard_map(
         per_device,

time: 40.7 us -> 35.1 us (0.86)
  Pallas kernels: 39.9 us -> 30.6 us
  local copies, waits for them, and re-layouts: 0 us -> 3.69 us
    pallas_call x1, Pallas kernels: 36.2 us -> 30.6 us  [per_device(): pl.pallas_call(functools.partial(kernel, nx, ny), out_shape=(jax.ShapeDty...]
    unnamed x0 -> x4, local copies, waits for them, and re-layouts: none -> 3.69 us
    pallas_call x1 -> x0, Pallas kernels: 3.69 us -> none  [per_device(): pl.pallas_call(copy_kernel, out_shape=(jax.ShapeDtypeStruct((cx, cy, cols...]
where the time goes in v3:
time: 35.1 us; the launch traced here: 34.9 us
  Pallas kernels  30.6 us (87%)
  local copies, waits for them, and re-layouts  3.69 us (11%)
  between operations  0.65 us (2%)
    pallas_call x1, Pallas kernels, per_device(): pl.pallas_call(functools.partial(kernel, nx, ny), out_shape=(jax.ShapeDty...  30.6 us
    unnamed x4, local copies, waits for them, and re-layouts  3.69 us

profile of v3, /device:TPU:0, one launch (start us, length us, event | category | flops | bytes accessed | tf_op | source)
XLA Modules:
  0.0 34.9 jit_solution(13826294816864227212)
XLA Ops:
  0.6 30.6 %shard_map.68 = (bf16[16,128,512]{2,1,0:T(8,128)(2,1)}, f32[2,512]{1,0:T(2,128)}) custom-call(bf16[16,128,512]{2,1,0:T(8,128)(2,1)} %adj.1, f32[16,128]{1,0:T(8,128)} %kx_ref.1, f32[16,128]{1,0:T(8,128)} %ky_ref.1, bf16[64,16,128]{2,1,0:T(8,128)(2,1)} %w_ref.1, s32[1,64]{1,0:T(1,128)} %bitcast.1), custom_call_target="tpu_custom_call" | custom-call | tf_op jit(solution)/shard_map/pallas_call | solution.py:351
  31.2 0.0 copy-start
  31.2 3.1 %copy.9 = bf16[16,128,512]{2,1,0:T(8,128)(2,1)} copy(bf16[16,128,512]{2,1,0:T(8,128)(2,1)} %get-tuple-element.4) | data formatting | bytes 4194304
  34.3 0.0 copy-done
  34.3 0.6 %copy.10 = f32[2,512]{1,0:T(2,128)} copy(f32[2,512]{1,0:T(2,128)S(1)} %copy-done) | data formatting | bytes 8192
Async XLA Ops:
  31.2 3.1 %copy-start = (f32[2,512]{1,0:T(2,128)S(1)}, f32[2,512]{1,0:T(2,128)}, u32[]{:S(2)}) copy-start(f32[2,512]{1,0:T(2,128)} %get-tuple-element.5) | copy-start | bytes 12292

commit v4 on v3

--- a/solution.py
+++ b/solution.py
@@ -148,12 +148,15 @@
 
     pl.semaphore_wait(barrier, n - 1)
 
+    order = [(d, 0, 2) for d in DIRS] + [(d, 2, 3) for d in DIRS[:6]]
+    order += [(d, 2 + q, 3 + q) for q in range(groups) for d in DIRS[6:]]
+    for (dx, dy), first, last in order:
+        @pl.when(present(dx, dy))
+        def _(dx=dx, dy=dy, first=first, last=last):
+            for c in copies(dx, dy)[first:last]:
+                c.start()
+
     for dx, dy in DIRS:
-        @pl.when(present(dx, dy))
-        def _(dx=dx, dy=dy):
-            for c in copies(dx, dy):
-                c.start()
-
         @pl.when(jnp.logical_not(present(dx, dy)))
         def _(dx=dx, dy=dy):
             part = region(dx, dy)
@@ -287,6 +290,7 @@
 
     for d in DIRS[2:6]:
         wait_recv(*d, "a")
+    middle = product(STEPS, cx - STEPS)
     for q in range(groups):
         for d in DIRS[6:]:
             wait_recv(*d, q)
@@ -299,7 +303,7 @@
 
     store = pltpu.make_async_copy(out, out_hbm, out_sem)
     store.start()
-    total = product(0, cx)
+    total = middle + product(0, STEPS) + product(cx - STEPS, cx)
     for q in range(groups):
         ps[pl.ds(q, picks, stride=groups), :] = total[:, q * LANES : (q + 1) * LANES]
 

time: 35.1 us -> 34.5 us (0.983)
  Pallas kernels: 30.6 us -> 30 us
    pallas_call x1, Pallas kernels: 30.6 us -> 30 us  [per_device(): pl.pallas_call(functools.partial(kernel, nx, ny), out_shape=(jax.ShapeDty...]
where the time goes in v4:
time: 34.5 us; the launch traced here: 34.3 us
  Pallas kernels  30 us (87%)
  local copies, waits for them, and re-layouts  3.69 us (11%)
  between operations  0.65 us (2%)
    pallas_call x1, Pallas kernels, per_device(): pl.pallas_call(functools.partial(kernel, nx, ny), out_shape=(jax.ShapeDty...  30 us
    unnamed x4, local copies, waits for them, and re-layouts  3.69 us

profile of v4, /device:TPU:0, one launch (start us, length us, event | category | flops | bytes accessed | tf_op | source)
XLA Modules:
  0.0 34.3 jit_solution(3193105194480692630)
XLA Ops:
  0.6 30.0 %shard_map.68 = (bf16[16,128,512]{2,1,0:T(8,128)(2,1)}, f32[2,512]{1,0:T(2,128)}) custom-call(bf16[16,128,512]{2,1,0:T(8,128)(2,1)} %adj.1, f32[16,128]{1,0:T(8,128)} %kx_ref.1, f32[16,128]{1,0:T(8,128)} %ky_ref.1, bf16[64,16,128]{2,1,0:T(8,128)(2,1)} %w_ref.1, s32[1,64]{1,0:T(1,128)} %bitcast.1), custom_call_target="tpu_custom_call" | custom-call | tf_op jit(solution)/shard_map/pallas_call | solution.py:355
  30.6 0.0 copy-start
  30.6 3.1 %copy.9 = bf16[16,128,512]{2,1,0:T(8,128)(2,1)} copy(bf16[16,128,512]{2,1,0:T(8,128)(2,1)} %get-tuple-element.4) | data formatting | bytes 4194304
  33.7 0.0 copy-done
  33.7 0.6 %copy.10 = f32[2,512]{1,0:T(2,128)} copy(f32[2,512]{1,0:T(2,128)S(1)} %copy-done) | data formatting | bytes 8192
Async XLA Ops:
  30.6 3.1 %copy-start = (f32[2,512]{1,0:T(2,128)S(1)}, f32[2,512]{1,0:T(2,128)}, u32[]{:S(2)}) copy-start(f32[2,512]{1,0:T(2,128)} %get-tuple-element.5) | copy-start | bytes 12292
